TPU v7x, 256 devices: a whole 4x4x8 slice. The times are simulated.
256 devices in a mesh: grp: 8 (over y, core), sub: 32 (over x, z).
Axes of the slice: x: 4, y: 4, z: 8, core: 2. Of those that a mesh axis runs over, the one named last changes fastest.
Arguments:
- cluster_pos: float32 [3, 4096], P(None, 'sub'), may hold values from -3 to 3
- cluster_vel: float32 [3, 4096], P(None, 'sub'), may hold values from -15 to 15
- cluster_mass: float32 [4096], P('sub'), may hold values from 3 to 60
- galaxy_pos: float32 [3, 131072], P(None, ('grp', 'sub')), may hold values from -1 to 7
- galaxy_vel: float32 [3, 131072], P(None, ('grp', 'sub')), may hold values from -3 to 3
- galaxy_kind: int32 [131072], P(('grp', 'sub')), may hold values from 0 to 3
- species_mass: float32 [4], replicated, may hold values from 10 to 80
Outputs:
- cluster_pos_out: float32 [3, 4096], P(None, 'sub')
- cluster_vel_out: float32 [3, 4096], P(None, 'sub')
- galaxy_pos_out: float32 [3, 131072], P(None, ('grp', 'sub'))
- galaxy_vel_out: float32 [3, 131072], P(None, ('grp', 'sub'))
All inputs are finite; a program needn't handle non-finite values.
Results may differ from a plain program's by a relative error of at most 0.0003.
Values sent between devices are 32-bit elements; how exact they have to be, the bound alone decides.
A program may use at most 64 MiB of HBM per device.

v0:
```python
import jax
import jax.numpy as jnp
from jax import lax
from jax.sharding import PartitionSpec as P

SUBSTEPS = 8
step_time = 0.5
bridge_soft = 0.01
cluster_soft = 0.0025
tile_limit = 524288


def pick_block(target_count, source_count):
    tile_size = target_count
    while tile_size > 1 and (
        tile_size * source_count > tile_limit or target_count % tile_size != 0
    ):
        tile_size = tile_size // 2
    return tile_size


def field(targets, sources, masses, soften):
    target_count = targets.shape[1]
    tile_size = pick_block(target_count, sources.shape[1])

    def field_one_tile(target_tile):
        separation = sources[:, None, :] - target_tile[:, :, None]
        distance = jnp.sum(separation * separation, axis=0) + soften
        inverse = lax.rsqrt(distance)
        weight = masses[None, :] * inverse * inverse * inverse
        return jnp.sum(separation * weight[None], axis=2)

    stacked = targets.reshape(3, target_count // tile_size, tile_size).transpose(1, 0, 2)
    result = lax.map(field_one_tile, stacked)
    return result.transpose(1, 0, 2).reshape(3, target_count)


def rates(target_pos, target_vel, source_pos, source_vel, masses, soften):
    target_count = target_pos.shape[1]
    tile_size = pick_block(target_count, source_pos.shape[1])

    def rates_one_tile(target_tile):
        separation = source_pos[:, None, :] - target_tile[:3, :, None]
        closing = source_vel[:, None, :] - target_tile[3:, :, None]
        distance = jnp.sum(separation * separation, axis=0) + soften
        inverse = lax.rsqrt(distance)
        weight = masses[None, :] * inverse * inverse * inverse
        radial = 3.0 * jnp.sum(separation * closing, axis=0) / distance
        acceleration = jnp.sum(separation * weight[None], axis=2)
        jerk_rate = jnp.sum((closing - radial[None] * separation) * weight[None], axis=2)
        return jnp.concatenate([acceleration, jerk_rate], axis=0)

    stacked = jnp.concatenate([target_pos, target_vel], axis=0)
    stacked = stacked.reshape(6, target_count // tile_size, tile_size).transpose(1, 0, 2)
    result = lax.map(rates_one_tile, stacked)
    return result.transpose(1, 0, 2).reshape(6, target_count)


def local(
    cluster_pos, cluster_vel, cluster_mass, galaxy_pos, galaxy_vel, galaxy_kind, species_mass
):
    star_count = cluster_pos.shape[1]
    member_count = lax.axis_size("sub")
    group_count = lax.axis_size("grp")
    total_stars = star_count * member_count
    total_bodies = galaxy_pos.shape[1] * member_count * group_count
    star_mass = cluster_mass / total_stars
    species = jnp.arange(species_mass.shape[0], dtype=jnp.int32)
    body_mass = (
        jnp.sum(
            jnp.where(galaxy_kind[None, :] == species[:, None], species_mass[:, None], 0.0), axis=0
        )
        / total_bodies
    )
    half_step = step_time / 2.0

    def kick(star_positions, body_positions):
        stacked = jnp.concatenate([star_positions, star_mass[None, :]], axis=0)
        gathered = lax.all_gather(stacked, "sub", axis=1, tiled=True)
        galaxy_push = field(body_positions, gathered[:3], gathered[3], bridge_soft)
        partial_value = field(gathered[:3], body_positions, body_mass, bridge_soft)
        summed = lax.psum(partial_value, ("grp", "sub"))
        cluster_pull = lax.dynamic_slice_in_dim(
            summed, lax.axis_index("sub") * star_count, star_count, 1
        )
        return (cluster_pull, galaxy_push)

    def evaluate(guess_pos, guess_vel):
        sources = jnp.concatenate([guess_pos, guess_vel, star_mass[None, :]], axis=0)
        target_pos, target_vel = (guess_pos, guess_vel)
        source_piece = lax.all_gather(sources, "sub", axis=1, tiled=True)
        result = rates(
            target_pos,
            target_vel,
            source_piece[:3],
            source_piece[3:6],
            source_piece[6],
            cluster_soft,
        )
        return (result[:3], result[3:])

    first_pull, first_push = kick(cluster_pos, galaxy_pos)
    star_vel = cluster_vel + half_step * first_pull
    body_vel = galaxy_vel + half_step * first_push
    body_pos = galaxy_pos + step_time * body_vel
    substep_time = step_time / SUBSTEPS
    positions, velocity = (cluster_pos, star_vel)
    acceleration, jerk_rate = evaluate(positions, velocity)
    for substep in range(SUBSTEPS):
        guess_pos = positions + substep_time * (
            velocity + substep_time * (acceleration / 2.0 + substep_time * jerk_rate / 6.0)
        )
        guess_vel = velocity + substep_time * (acceleration + substep_time * jerk_rate / 2.0)
        new_acc, new_jerk = evaluate(guess_pos, guess_vel)
        new_vel = (
            velocity
            + substep_time / 2.0 * (acceleration + new_acc)
            + substep_time * substep_time / 12.0 * (jerk_rate - new_jerk)
        )
        new_pos = (
            positions
            + substep_time / 2.0 * (velocity + new_vel)
            + substep_time * substep_time / 12.0 * (acceleration - new_acc)
        )
        positions, velocity, acceleration, jerk_rate = (new_pos, new_vel, new_acc, new_jerk)
    second_pull, second_push = kick(positions, body_pos)
    return (
        positions,
        velocity + half_step * second_pull,
        body_pos,
        body_vel + half_step * second_push,
    )


def solution(mesh):
    return jax.shard_map(
        local,
        mesh=mesh,
        in_specs=(
            P(None, "sub"),
            P(None, "sub"),
            P("sub"),
            P(None, ("grp", "sub")),
            P(None, ("grp", "sub")),
            P(("grp", "sub")),
            P(),
        ),
        out_specs=(
            P(None, "sub"),
            P(None, "sub"),
            P(None, ("grp", "sub")),
            P(None, ("grp", "sub")),
        ),
        check_vma=False,
    )
```

profile of v0, /device:TPU:1, one launch (start us, length us, event | category | flops | bytes accessed | tf_op | source)
XLA Modules:
  0.0 715.4 jit_solution(4176489332510097580)
XLA Ops:
  2.0 40.5 %all_gather.33 = f32[4,4096]{1,0:T(4,128)S(1)} all-gather(f32[4,128]{1,0:T(4,128)S(1)} %pad_maximum_fusion.10), channel_id=1, replica_groups=mesh['grp'=8,'sub'=32] {'sub'}, dimensions={1}, use_global_device_ids=true | all-gather | bytes 67584 | tf_op jit(solution)/shard_map/all_gather | solution.py:79
  43.3 14.5 %while.8 = (s32[]{:T(128)}, f32[4,3,1024]{2,1,0:T(4,128)S(1)}, f32[3,512]{1,0:T(4,128)}, f32[4,3,1024]{2,1,0:T(4,128)S(1)}, f32[512]{0:T(512)S(1)}, /*index=5*/s32[]{:T(128)}) while((s32[]{:T(128)}, f32[4,3,1024]{2,1,0:T(4,128)S(1)}, f32[3,512]{1,0:T(4,128)}, f32[4,3,1024]{2,1,0:T(4,128)S(1)}, f32[512]{0:T(512)S(1)}, ...), condition=%wide.region_4.5_spmd, body=%wide.region_1.4_spmd.sunk | while | flops 11006978 | bytes 8521833 | solution.py:34
  43.3 1.6 fusion.70
  45.6 1.2 fusion.71
  46.9 1.6 fusion.70
  49.3 1.2 fusion.71
  50.5 1.6 fusion.70
  52.9 1.2 fusion.71
  54.2 1.6 fusion.70
  56.5 1.2 fusion.71
  57.8 87.6 %psum.14 = f32[3,4096]{1,0:T(4,128)S(1)} all-reduce(f32[3,4096]{1,0:T(4,128)S(1)} %bitcast.93), channel_id=1, replica_groups=mesh['grp'=8,'sub'=32] {'grp','sub'}, use_global_device_ids=true, to_apply=%region_5.6 | all-reduce | flops 12288 | bytes 98304 | tf_op jit(solution)/shard_map/psum | solution.py:82
  145.4 31.0 %all_gather.34 = f32[7,4096]{1,0:T(8,128)S(1)} all-gather(f32[7,128]{1,0:T(8,128)S(1)} %pad_maximum_fusion.8), channel_id=1, replica_groups=mesh['grp'=8,'sub'=32] {'sub'}, dimensions={1}, use_global_device_ids=true | all-gather | bytes 118272 | tf_op jit(solution)/shard_map/all_gather | solution.py:91
  176.4 1.9 fusion.26
  179.0 2.1 fusion.27
  181.2 32.3 %all_gather.35 = f32[7,4096]{1,0:T(8,128)S(1)} all-gather(f32[7,128]{1,0:T(8,128)S(1)} %pad_maximum_fusion.7), channel_id=1, replica_groups=mesh['grp'=8,'sub'=32] {'sub'}, dimensions={1}, use_global_device_ids=true | all-gather | bytes 118272 | tf_op jit(solution)/shard_map/all_gather | solution.py:91
  213.5 2.0 fusion.31
  216.2 2.2 fusion.11
  218.4 31.8 %all_gather.36 = f32[7,4096]{1,0:T(8,128)S(1)} all-gather(f32[7,128]{1,0:T(8,128)S(1)} %pad_maximum_fusion.6), channel_id=1, replica_groups=mesh['grp'=8,'sub'=32] {'sub'}, dimensions={1}, use_global_device_ids=true | all-gather | bytes 118272 | tf_op jit(solution)/shard_map/all_gather | solution.py:91
  250.2 2.0 fusion.34
  252.9 2.2 fusion.13
  255.1 33.7 %all_gather.37 = f32[7,4096]{1,0:T(8,128)S(1)} all-gather(f32[7,128]{1,0:T(8,128)S(1)} %pad_maximum_fusion.5), channel_id=1, replica_groups=mesh['grp'=8,'sub'=32] {'sub'}, dimensions={1}, use_global_device_ids=true | all-gather | bytes 118272 | tf_op jit(solution)/shard_map/all_gather | solution.py:91
  288.9 2.0 fusion.37
  291.5 2.2 fusion.15
  293.7 30.9 %all_gather.38 = f32[7,4096]{1,0:T(8,128)S(1)} all-gather(f32[7,128]{1,0:T(8,128)S(1)} %pad_maximum_fusion.4), channel_id=1, replica_groups=mesh['grp'=8,'sub'=32] {'sub'}, dimensions={1}, use_global_device_ids=true | all-gather | bytes 118272 | tf_op jit(solution)/shard_map/all_gather | solution.py:91
  324.6 2.0 fusion.40
  327.3 2.2 fusion.17
  329.5 33.5 %all_gather.39 = f32[7,4096]{1,0:T(8,128)S(1)} all-gather(f32[7,128]{1,0:T(8,128)S(1)} %pad_maximum_fusion.3), channel_id=1, replica_groups=mesh['grp'=8,'sub'=32] {'sub'}, dimensions={1}, use_global_device_ids=true | all-gather | bytes 118272 | tf_op jit(solution)/shard_map/all_gather | solution.py:91
  363.0 2.0 fusion.43
  365.7 2.2 fusion.19
  367.9 30.7 %all_gather.40 = f32[7,4096]{1,0:T(8,128)S(1)} all-gather(f32[7,128]{1,0:T(8,128)S(1)} %pad_maximum_fusion.2), channel_id=1, replica_groups=mesh['grp'=8,'sub'=32] {'sub'}, dimensions={1}, use_global_device_ids=true | all-gather | bytes 118272 | tf_op jit(solution)/shard_map/all_gather | solution.py:91
  398.6 2.0 fusion.46
  401.3 2.2 fusion.21
  403.5 33.4 %all_gather.41 = f32[7,4096]{1,0:T(8,128)S(1)} all-gather(f32[7,128]{1,0:T(8,128)S(1)} %pad_maximum_fusion.1), channel_id=1, replica_groups=mesh['grp'=8,'sub'=32] {'sub'}, dimensions={1}, use_global_device_ids=true | all-gather | bytes 118272 | tf_op jit(solution)/shard_map/all_gather | solution.py:91
  437.0 2.0 fusion.49
  439.6 2.2 fusion.23
  441.8 31.1 %all_gather.42 = f32[7,4096]{1,0:T(8,128)S(1)} all-gather(f32[7,128]{1,0:T(8,128)S(1)} %pad_maximum_fusion), channel_id=1, replica_groups=mesh['grp'=8,'sub'=32] {'sub'}, dimensions={1}, use_global_device_ids=true | all-gather | bytes 118272 | tf_op jit(solution)/shard_map/all_gather | solution.py:91
  473.0 2.0 fusion.52
  475.6 2.2 fusion.25
  477.9 36.5 %all_gather.43 = f32[4,4096]{1,0:T(4,128)S(1)} all-gather(f32[4,128]{1,0:T(4,128)S(1)} %pad_maximum_fusion.9), channel_id=1, replica_groups=mesh['grp'=8,'sub'=32] {'sub'}, dimensions={1}, use_global_device_ids=true | all-gather | bytes 67584 | tf_op jit(solution)/shard_map/all_gather | solution.py:79
  514.4 8.5 %while.9 = (s32[]{:T(128)}, f32[4,3,128]{2,1,0:T(4,128)S(1)}, f32[3,4096]{1,0:T(4,128)S(1)}, f32[4,3,128]{2,1,0:T(4,128)S(1)}, f32[1,4096]{1,0:T(1,128)S(1)}, /*index=5*/s32[]{:T(128)}) while((s32[]{:T(128)}, f32[4,3,128]{2,1,0:T(4,128)S(1)}, f32[3,4096]{1,0:T(4,128)S(1)}, f32[4,3,128]{2,1,0:T(4,128)S(1)}, f32[1,4096]{1,0:T(1,128)S(1)}, ...), condition=%wide.region_45.46_spmd, body=%wide.region_42.45_spmd.sunk | while | flops 11009666 | bytes 8515149 | solution.py:34
  514.5 0.9 fusion.72
  515.7 0.8 fusion.73
  516.6 0.9 fusion.72
  517.8 0.8 fusion.73
  518.7 0.9 fusion.72
  519.9 0.8 fusion.73
  520.8 0.9 fusion.72
  522.1 0.8 fusion.73
  523.0 8.5 %while.11 = (s32[]{:T(128)}, f32[4,3,128]{2,1,0:T(4,128)S(1)}, f32[3,4096]{1,0:T(4,128)S(1)}, f32[4,3,128]{2,1,0:T(4,128)S(1)}, f32[1,4096]{1,0:T(1,128)S(1)}, /*index=5*/s32[]{:T(128)}) while((s32[]{:T(128)}, f32[4,3,128]{2,1,0:T(4,128)S(1)}, f32[3,4096]{1,0:T(4,128)S(1)}, f32[4,3,128]{2,1,0:T(4,128)S(1)}, f32[1,4096]{1,0:T(1,128)S(1)}, ...), condition=%wide.region_54.55_spmd, body=%wide.region_51.54_spmd.sunk | while | flops 11009666 | bytes 8515149 | solution.py:34
  523.0 0.9 fusion.76
  525.1 0.9 fusion.76
  527.2 0.9 fusion.76
  529.4 0.9 fusion.76
  530.6 0.8 fusion.77
  532.1 10.4 %while.10 = (s32[]{:T(128)}, f32[4,3,1024]{2,1,0:T(4,128)S(1)}, f32[3,512]{1,0:T(4,128)S(1)}, f32[4,3,1024]{2,1,0:T(4,128)S(1)}, f32[512]{0:T(512)S(1)}, /*index=5*/s32[]{:T(128)}) while((s32[]{:T(128)}, f32[4,3,1024]{2,1,0:T(4,128)S(1)}, f32[3,512]{1,0:T(4,128)S(1)}, f32[4,3,1024]{2,1,0:T(4,128)S(1)}, f32[512]{0:T(512)S(1)}, ...), condition=%wide.region_49.50_spmd, body=%wide.region_46.49_spmd.sunk | while | flops 11006978 | bytes 8497229 | solution.py:34
  532.1 0.9 fusion.74
  533.4 1.2 fusion.75
  534.7 0.9 fusion.74
  536.0 1.2 fusion.75
  537.3 0.9 fusion.74
  538.6 1.2 fusion.75
  539.9 0.9 fusion.74
  541.2 1.2 fusion.75
  542.5 171.9 %psum.15 = f32[3,4096]{1,0:T(4,128)S(1)} all-reduce(f32[3,4096]{1,0:T(4,128)S(1)} %bitcast.92), channel_id=1, replica_groups=mesh['grp'=8,'sub'=32] {'grp','sub'}, use_global_device_ids=true, to_apply=%region_50.51 | all-reduce | flops 12288 | bytes 98304 | tf_op jit(solution)/shard_map/psum | solution.py:82
  (134 shorter events, 18.9 us)
Async XLA Ops:
  43.2 102.1 %copy-start.6 = (f32[3,128]{1,0:T(4,128)S(1)}, f32[3,128]{1,0:T(4,128)}, u32[]{:S(2)}) copy-start(f32[3,128]{1,0:T(4,128)} %param.16) | copy-start | bytes 4612
  43.2 102.1 %copy-start.3 = (f32[3,128]{1,0:T(4,128)S(1)}, f32[3,128]{1,0:T(4,128)}, u32[]{:S(2)}) copy-start(f32[3,128]{1,0:T(4,128)} %param.15) | copy-start | bytes 4612
  44.9 0.7 copy-start
  48.6 0.7 copy-start
  52.2 0.7 copy-start
  55.8 0.7 copy-start
  475.6 38.8 %copy-start.1 = (f32[3,512]{1,0:T(4,128)S(1)}, f32[3,512]{1,0:T(4,128)}, u32[]{:S(2)}) copy-start(f32[3,512]{1,0:T(4,128)} %get-tuple-element.607) | copy-start | bytes 18436
  477.8 36.6 %copy-start.5 = (f32[3,128]{1,0:T(4,128)}, f32[3,128]{1,0:T(4,128)S(1)}, u32[]{:S(2)}) copy-start(f32[3,128]{1,0:T(4,128)S(1)} %multiply_add_fusion.2) | copy-start | bytes 4612
  514.4 8.5 %copy-start.4 = (f32[3,512]{1,0:T(4,128)S(1)}, f32[3,512]{1,0:T(4,128)}, u32[]{:S(2)}) copy-start(f32[3,512]{1,0:T(4,128)} %param.19) | copy-start | bytes 18436
  542.5 172.5 %copy-start.2 = (f32[3,512]{1,0:T(4,128)}, f32[3,512]{1,0:T(4,128)S(1)}, u32[]{:S(2)}) copy-start(f32[3,512]{1,0:T(4,128)S(1)} %get-tuple-element.610) | copy-start | bytes 18436
where the time goes:
time: 725 us; the launch traced here: 715 us
  blocking collectives  625 us (86%)
  other arithmetic  86 us (12%)
    all_gather x9, blocking collectives, evaluate(): source_piece = lax.all_gather(sources, 'sub', axis=1, tiled=True)  288 us
    psum x2, blocking collectives, kick(): summed = lax.psum(partial_value, ('grp', 'sub'))  259 us
    all_gather x2, blocking collectives, kick(): gathered = lax.all_gather(stacked, 'sub', axis=1, tiled=True)  76.9 us
    reduce_sum x8, other arithmetic, rates_one_tile(): jnp.sum((closing - radial[None] * separation) * weight[None], axis=2)  17.5 us
    reduce_sum x16, other arithmetic, field_one_tile(): distance = jnp.sum(separation * separation, axis=0) + soften  17.3 us
    reduce_sum x16, other arithmetic, field_one_tile(): return jnp.sum(separation * weight[None], axis=2)  16.5 us
    reduce_sum x8, other arithmetic, rates_one_tile(): radial = 3.0 * jnp.sum(separation * closing, axis=0) / distance  16.4 us

commit v1 on v0

--- a/solution.py
+++ b/solution.py
@@ -76,7 +76,7 @@
 
     def kick(star_positions, body_positions):
         stacked = jnp.concatenate([star_positions, star_mass[None, :]], axis=0)
-        gathered = lax.all_gather(stacked, "sub", axis=1, tiled=True)
+        gathered = jnp.concatenate(lax.all_gather(stacked, axis_name="sub"), 1)
         galaxy_push = field(body_positions, gathered[:3], gathered[3], bridge_soft)
         partial_value = field(gathered[:3], body_positions, body_mass, bridge_soft)
         summed = lax.psum(partial_value, ("grp", "sub"))

time: 725 us -> 727 us (level)
  no operation moved by 1% of the time
where the time goes in v1:
time: 727 us; the launch traced here: 719 us
  blocking collectives  625 us (86%)
  other arithmetic  86.7 us (12%)
    all_gather x9, blocking collectives, evaluate(): source_piece = lax.all_gather(sources, 'sub', axis=1, tiled=True)  289 us
    psum x2, blocking collectives, kick(): summed = lax.psum(partial_value, ('grp', 'sub'))  261 us
    all_gather x2, blocking collectives, kick(): gathered = jnp.concatenate(lax.all_gather(stacked, axis_name='sub'), 1)  74.7 us
    reduce_sum x8, other arithmetic, rates_one_tile(): jnp.sum((closing - radial[None] * separation) * weight[None], axis=2)  17.5 us
    reduce_sum x16, other arithmetic, field_one_tile(): distance = jnp.sum(separation * separation, axis=0) + soften  17.3 us
    reduce_sum x16, other arithmetic, field_one_tile(): return jnp.sum(separation * weight[None], axis=2)  16.5 us
    reduce_sum x8, other arithmetic, rates_one_tile(): radial = 3.0 * jnp.sum(separation * closing, axis=0) / distance  16.4 us

profile of v1, /device:TPU:1, one launch (start us, length us, event | category | flops | bytes accessed | tf_op | source)
XLA Modules:
  0.0 719.3 jit_solution(8340239563741090129)
XLA Ops:
  2.8 40.5 %all-gather.2 = f32[32,4,128]{2,1,0:T(4,128)S(1)} all-gather(f32[1,4,128]{2,1,0:T(4,128)S(1)} %fusion.53), channel_id=2, replica_groups=mesh['grp'=8,'sub'=32] {'sub'}, dimensions={0}, use_global_device_ids=true | all-gather | bytes 67584 | tf_op jit(solution)/shard_map/all_gather | solution.py:79
  43.3 14.5 %while.8 = (s32[]{:T(128)}, f32[4,3,1024]{2,1,0:T(4,128)S(1)}, f32[3,512]{1,0:T(4,128)}, f32[4,3,1024]{2,1,0:T(4,128)S(1)}, f32[512]{0:T(512)S(1)}, /*index=5*/s32[]{:T(128)}) while((s32[]{:T(128)}, f32[4,3,1024]{2,1,0:T(4,128)S(1)}, f32[3,512]{1,0:T(4,128)}, f32[4,3,1024]{2,1,0:T(4,128)S(1)}, f32[512]{0:T(512)S(1)}, ...), condition=%wide.region_4.5_spmd, body=%wide.region_1.4_spmd.sunk | while | flops 11006978 | bytes 8521841 | solution.py:34
  43.3 1.6 fusion.72
  45.7 1.2 fusion.73
  47.0 1.6 fusion.72
  49.3 1.2 fusion.73
  50.6 1.6 fusion.72
  52.9 1.2 fusion.73
  54.2 1.6 fusion.72
  56.6 1.2 fusion.73
  57.8 87.6 %psum.14 = f32[3,4096]{1,0:T(4,128)S(1)} all-reduce(f32[3,4096]{1,0:T(4,128)S(1)} %bitcast.105), channel_id=1, replica_groups=mesh['grp'=8,'sub'=32] {'grp','sub'}, use_global_device_ids=true, to_apply=%region_5.6 | all-reduce | flops 12288 | bytes 98304 | tf_op jit(solution)/shard_map/psum | solution.py:82
  145.4 11.2 %while.9 = (s32[]{:T(128)}, f32[4,3,128]{2,1,0:T(4,128)S(1)}, f32[3,4096]{1,0:T(4,128)S(1)}, f32[4,3,128]{2,1,0:T(4,128)}, f32[1,4096]{1,0:T(1,128)S(1)}, /*index=5*/s32[]{:T(128)}) while((s32[]{:T(128)}, f32[4,3,128]{2,1,0:T(4,128)S(1)}, f32[3,4096]{1,0:T(4,128)S(1)}, f32[4,3,128]{2,1,0:T(4,128)}, f32[1,4096]{1,0:T(1,128)S(1)}, ...), condition=%wide.region_45.46_spmd, body=%wide.region_42.45_spmd.sunk | while | flops 11009666 | bytes 8515157 | solution.py:34
  146.1 0.9 fusion.74
  147.4 0.8 fusion.75
  148.9 0.9 fusion.74
  150.1 0.8 fusion.75
  151.7 0.9 fusion.74
  152.9 0.8 fusion.75
  154.5 0.9 fusion.74
  155.7 0.8 fusion.75
  157.4 31.0 %all_gather.41 = f32[7,4096]{1,0:T(8,128)S(1)} all-gather(f32[7,128]{1,0:T(8,128)S(1)} %pad_maximum_fusion.8), channel_id=1, replica_groups=mesh['grp'=8,'sub'=32] {'sub'}, dimensions={1}, use_global_device_ids=true | all-gather | bytes 118272 | tf_op jit(solution)/shard_map/all_gather | solution.py:91
  188.4 1.9 fusion.26
  191.0 2.1 fusion.27
  193.1 32.9 %all_gather.42 = f32[7,4096]{1,0:T(8,128)S(1)} all-gather(f32[7,128]{1,0:T(8,128)S(1)} %pad_maximum_fusion.7), channel_id=1, replica_groups=mesh['grp'=8,'sub'=32] {'sub'}, dimensions={1}, use_global_device_ids=true | all-gather | bytes 118272 | tf_op jit(solution)/shard_map/all_gather | solution.py:91
  226.1 2.0 fusion.31
  228.7 2.2 fusion.11
  230.9 31.3 %all_gather.43 = f32[7,4096]{1,0:T(8,128)S(1)} all-gather(f32[7,128]{1,0:T(8,128)S(1)} %pad_maximum_fusion.6), channel_id=1, replica_groups=mesh['grp'=8,'sub'=32] {'sub'}, dimensions={1}, use_global_device_ids=true | all-gather | bytes 118272 | tf_op jit(solution)/shard_map/all_gather | solution.py:91
  262.3 2.0 fusion.34
  264.9 2.2 fusion.13
  267.1 33.8 %all_gather.44 = f32[7,4096]{1,0:T(8,128)S(1)} all-gather(f32[7,128]{1,0:T(8,128)S(1)} %pad_maximum_fusion.5), channel_id=1, replica_groups=mesh['grp'=8,'sub'=32] {'sub'}, dimensions={1}, use_global_device_ids=true | all-gather | bytes 118272 | tf_op jit(solution)/shard_map/all_gather | solution.py:91
  300.9 2.0 fusion.37
  303.6 2.2 fusion.15
  305.8 30.5 %all_gather.45 = f32[7,4096]{1,0:T(8,128)S(1)} all-gather(f32[7,128]{1,0:T(8,128)S(1)} %pad_maximum_fusion.4), channel_id=1, replica_groups=mesh['grp'=8,'sub'=32] {'sub'}, dimensions={1}, use_global_device_ids=true | all-gather | bytes 118272 | tf_op jit(solution)/shard_map/all_gather | solution.py:91
  336.4 2.0 fusion.40
  339.0 2.2 fusion.17
  341.3 33.2 %all_gather.46 = f32[7,4096]{1,0:T(8,128)S(1)} all-gather(f32[7,128]{1,0:T(8,128)S(1)} %pad_maximum_fusion.3), channel_id=1, replica_groups=mesh['grp'=8,'sub'=32] {'sub'}, dimensions={1}, use_global_device_ids=true | all-gather | bytes 118272 | tf_op jit(solution)/shard_map/all_gather | solution.py:91
  374.5 2.0 fusion.43
  377.1 2.2 fusion.19
  379.3 31.3 %all_gather.47 = f32[7,4096]{1,0:T(8,128)S(1)} all-gather(f32[7,128]{1,0:T(8,128)S(1)} %pad_maximum_fusion.2), channel_id=1, replica_groups=mesh['grp'=8,'sub'=32] {'sub'}, dimensions={1}, use_global_device_ids=true | all-gather | bytes 118272 | tf_op jit(solution)/shard_map/all_gather | solution.py:91
  410.7 2.0 fusion.46
  413.3 2.2 fusion.21
  415.6 32.4 %all_gather.48 = f32[7,4096]{1,0:T(8,128)S(1)} all-gather(f32[7,128]{1,0:T(8,128)S(1)} %pad_maximum_fusion.1), channel_id=1, replica_groups=mesh['grp'=8,'sub'=32] {'sub'}, dimensions={1}, use_global_device_ids=true | all-gather | bytes 118272 | tf_op jit(solution)/shard_map/all_gather | solution.py:91
  448.1 2.0 fusion.49
  450.7 2.2 fusion.23
  452.9 32.9 %all_gather.49 = f32[7,4096]{1,0:T(8,128)S(1)} all-gather(f32[7,128]{1,0:T(8,128)S(1)} %pad_maximum_fusion), channel_id=1, replica_groups=mesh['grp'=8,'sub'=32] {'sub'}, dimensions={1}, use_global_device_ids=true | all-gather | bytes 118272 | tf_op jit(solution)/shard_map/all_gather | solution.py:91
  485.8 2.0 fusion.52
  488.4 2.2 fusion.25
  490.7 34.2 %all-gather.3 = f32[32,4,128]{2,1,0:T(4,128)S(1)} all-gather(f32[1,4,128]{2,1,0:T(4,128)S(1)} %fusion.54), channel_id=3, replica_groups=mesh['grp'=8,'sub'=32] {'sub'}, dimensions={0}, use_global_device_ids=true | all-gather | bytes 67584 | tf_op jit(solution)/shard_map/all_gather | solution.py:79
  525.0 10.4 %while.10 = (s32[]{:T(128)}, f32[4,3,1024]{2,1,0:T(4,128)S(1)}, f32[3,512]{1,0:T(4,128)S(1)}, f32[4,3,1024]{2,1,0:T(4,128)S(1)}, f32[512]{0:T(512)S(1)}, /*index=5*/s32[]{:T(128)}) while((s32[]{:T(128)}, f32[4,3,1024]{2,1,0:T(4,128)S(1)}, f32[3,512]{1,0:T(4,128)S(1)}, f32[4,3,1024]{2,1,0:T(4,128)S(1)}, f32[512]{0:T(512)S(1)}, ...), condition=%wide.region_49.50_spmd, body=%wide.region_46.49_spmd.sunk | while | flops 11006978 | bytes 8497237 | solution.py:34
  525.0 0.9 fusion.76
  526.3 1.2 fusion.77
  527.6 0.9 fusion.76
  528.9 1.2 fusion.77
  530.2 0.9 fusion.76
  531.5 1.2 fusion.77
  532.8 0.9 fusion.76
  534.1 1.2 fusion.77
  535.4 173.7 %psum.15 = f32[3,4096]{1,0:T(4,128)S(1)} all-reduce(f32[3,4096]{1,0:T(4,128)S(1)} %bitcast.106), channel_id=1, replica_groups=mesh['grp'=8,'sub'=32] {'grp','sub'}, use_global_device_ids=true, to_apply=%region_50.51 | all-reduce | flops 12288 | bytes 98304 | tf_op jit(solution)/shard_map/psum | solution.py:82
  709.7 8.5 %while.11 = (s32[]{:T(128)}, f32[4,3,128]{2,1,0:T(4,128)S(1)}, f32[3,4096]{1,0:T(4,128)S(1)}, f32[4,3,128]{2,1,0:T(4,128)S(1)}, f32[1,4096]{1,0:T(1,128)S(1)}, /*index=5*/s32[]{:T(128)}) while((s32[]{:T(128)}, f32[4,3,128]{2,1,0:T(4,128)S(1)}, f32[3,4096]{1,0:T(4,128)S(1)}, f32[4,3,128]{2,1,0:T(4,128)S(1)}, f32[1,4096]{1,0:T(1,128)S(1)}, ...), condition=%wide.region_54.55_spmd, body=%wide.region_51.54_spmd.sunk | while | flops 11009666 | bytes 8515157 | solution.py:34
  709.7 0.9 fusion.78
  710.9 0.8 fusion.79
  711.8 0.9 fusion.78
  714.0 0.9 fusion.78
  716.1 0.9 fusion.78
  (134 shorter events, 22.4 us)
Async XLA Ops:
  43.3 102.1 %copy-start.5 = (f32[3,128]{1,0:T(4,128)S(1)}, f32[3,128]{1,0:T(4,128)}, u32[]{:S(2)}) copy-start(f32[3,128]{1,0:T(4,128)} %param.16) | copy-start | bytes 4612
  45.0 0.7 copy-start
  48.6 0.7 copy-start
  52.2 0.7 copy-start
  55.9 0.7 copy-start
  145.4 11.2 %copy-start.2 = (f32[3,128]{1,0:T(4,128)S(1)}, f32[3,128]{1,0:T(4,128)}, u32[]{:S(2)}) copy-start(f32[3,128]{1,0:T(4,128)} %param.15) | copy-start | bytes 4612
  145.4 11.2 %copy-start.3 = (f32[3,512]{1,0:T(4,128)S(1)}, f32[3,512]{1,0:T(4,128)}, u32[]{:S(2)}) copy-start(f32[3,512]{1,0:T(4,128)} %param.19) | copy-start | bytes 18436
  490.7 34.3 %copy-start.4 = (f32[3,128]{1,0:T(4,128)}, f32[3,128]{1,0:T(4,128)S(1)}, u32[]{:S(2)}) copy-start(f32[3,128]{1,0:T(4,128)S(1)} %multiply_add_fusion.2) | copy-start | bytes 4612
  718.2 0.6 copy-start.1
